TPU v7x, 32 devices: a whole 2x2x4 slice. The times are simulated.
32 devices in a mesh: cell: 4 (over y, x), chan: 8 (over z, core).
Axes of the slice: x: 2, y: 2, z: 4, core: 2. Of those that a mesh axis runs over, the one named last changes fastest.
Arguments:
- slab: bfloat16 [32768, 8192], P('cell', 'chan'), may hold values from -6 to 6
- cell_factor: float32 [32, 32768], P(None, 'cell'), may hold values from -6 to 6
- chan_factor: float32 [32, 8192], P(None, 'chan'), may hold values from -6 to 6
- cell_mttkrp: float32 [32, 32768], P(None, 'cell'), may hold values from -12 to 12
- chan_mttkrp: float32 [32, 8192], P(None, 'chan'), may hold values from -12 to 12
- cell_gram_acc: float32 [32, 32], replicated, as said below
- chan_gram_acc: float32 [32, 32], replicated, as said below
Outputs:
- time_row: float32 [32], replicated
- new_cell_factor: float32 [32, 32768], P(None, 'cell')
- new_chan_factor: float32 [32, 8192], P(None, 'chan')
- new_cell_mttkrp: float32 [32, 32768], P(None, 'cell')
- new_chan_mttkrp: float32 [32, 8192], P(None, 'chan')
- new_cell_gram: float32 [32, 32], replicated
- new_chan_gram: float32 [32, 32], replicated
Inputs may be any that keep to these rules, and one draw needn't show every extreme that they name: `cell_gram_acc`: symmetric with a dominant positive diagonal. `chan_gram_acc`: symmetric with a dominant positive diagonal.
All inputs are finite; a program needn't handle non-finite values.
Results may differ from a plain program's by a relative error of at most 0.0033.
Values sent between devices are 32-bit elements; how exact they have to be, the bound alone decides.
No kernel may reach another device: no remote copies, remote signals or barrier semaphores. Data moves between devices by JAX's collectives and lax.ppermute only.
A program may use at most 64 MiB of HBM per device.

v0:
```python
import math
import jax
import jax.numpy as jnp
from jax import lax
from jax.sharding import PartitionSpec as P


def spd_solve(matrix, right):
    lower = jnp.linalg.cholesky(matrix)
    return jax.scipy.linalg.cho_solve((lower, True), right)


def body(slab, cell_factor, chan_factor, cell_mttkrp, chan_mttkrp, cell_gram_acc, chan_gram_acc):
    hi = lax.Precision.HIGHEST
    n_cell = lax.axis_size("cell")
    n_chan = lax.axis_size("chan")
    local_rows = slab.shape[0]
    local_cols = slab.shape[1]
    all_rows = local_rows * n_cell
    all_cols = local_cols * n_chan
    chan_low = chan_factor.astype(jnp.bfloat16)
    slab_chan = lax.dot_general(
        chan_low, slab, (((1,), (1,)), ((), ())), preferred_element_type=jnp.float32
    )
    rhs_part = jnp.sum(cell_factor * slab_chan, axis=1) / math.sqrt(all_rows * all_cols)
    cell_part = jnp.dot(cell_factor, cell_factor.T, precision=hi) / all_rows
    chan_part = jnp.dot(chan_factor, chan_factor.T, precision=hi) / all_cols
    rhs = lax.psum(rhs_part, ("cell", "chan"))
    cell_norm = lax.psum(cell_part, "cell")
    chan_norm = lax.psum(chan_part, "chan")
    time_row = spd_solve(cell_norm * chan_norm, rhs[:, None])[:, 0]
    outer = time_row[:, None] * time_row[None, :]
    new_cell_gram = cell_gram_acc + chan_norm * outer
    summed = lax.psum(slab_chan, "chan")
    new_cell_mttkrp = cell_mttkrp + time_row[:, None] * summed / math.sqrt(all_cols)
    new_cell_factor = spd_solve(new_cell_gram, new_cell_mttkrp)
    local_gram = jnp.dot(new_cell_factor, new_cell_factor.T, precision=hi) / all_rows
    new_norm = lax.psum(local_gram, "cell")
    cell_low = new_cell_factor.astype(jnp.bfloat16)
    slab_cell = jnp.dot(cell_low, slab, preferred_element_type=jnp.float32)
    cell_summed = lax.psum(slab_cell, "cell")
    new_chan_mttkrp = chan_mttkrp + time_row[:, None] * cell_summed / math.sqrt(all_rows)
    new_chan_gram = chan_gram_acc + new_norm * outer
    new_chan_factor = spd_solve(new_chan_gram, new_chan_mttkrp)
    return (
        time_row,
        new_cell_factor,
        new_chan_factor,
        new_cell_mttkrp,
        new_chan_mttkrp,
        new_cell_gram,
        new_chan_gram,
    )


def solution(mesh):
    placed = (
        P("cell", "chan"),
        P(None, "cell"),
        P(None, "chan"),
        P(None, "cell"),
        P(None, "chan"),
        P(),
        P(),
    )
    return jax.shard_map(
        body,
        mesh=mesh,
        in_specs=placed,
        out_specs=(
            P(),
            P(None, "cell"),
            P(None, "chan"),
            P(None, "cell"),
            P(None, "chan"),
            P(),
            P(),
        ),
        check_vma=False,
    )
```

profile of v0, /device:TPU:0, one launch (start us, length us, event | category | flops | bytes accessed | tf_op | source)
XLA Modules:
  0.0 202.9 jit_solution(13627783786792271417)
XLA Ops:
  7.3 12.4 %multiply_reduce_fusion = (f32[32]{0:T(128)S(1)}, f32[32,8192]{1,0:T(8,128)}) fusion(f32[32,8192]{1,0:T(8,128)} %param.9, bf16[8192,1024]{1,0:T(8,128)(2,1)} %param.8, f32[32,1024]{1,0:T(8,128)} %param.10), kind=kOutput, calls=%fused_computation.6 | convolution fusion | flops 537427968 | bytes 19005568 | tf_op jit(solution)/shard_map/dot_general | solution.py:22
  19.7 0.2 convolution_multiply_fusion.1
  20.0 1.0 convolution_multiply_fusion.2
  21.0 30.4 %psum.43 = f32[32,32]{0,1:T(8,128)S(1)} all-reduce(f32[32,32]{0,1:T(8,128)S(1)} %convolution_multiply_fusion.1), channel_id=1, replica_groups=mesh['cell'=4,'chan'=8] {'chan'}, use_global_device_ids=true, to_apply=%region_1.0 | all-reduce | flops 1024 | bytes 8192 | tf_op jit(solution)/shard_map/psum | solution.py:30
  51.3 16.0 %psum.42 = f32[32,32]{0,1:T(8,128)S(1)} all-reduce(f32[32,32]{0,1:T(8,128)S(1)} %convolution_multiply_fusion.2), channel_id=1, replica_groups=mesh['cell'=4,'chan'=8] {'cell'}, use_global_device_ids=true, to_apply=%region_0.0 | all-reduce | flops 1024 | bytes 8192 | tf_op jit(solution)/shard_map/psum | solution.py:29
  67.4 2.9 %cholesky.59 = f32[32,32]{1,0:T(8,128)S(1)} custom-call(f32[32,32]{1,0:T(8,128)S(1)} %fusion.21), custom_call_target="Cholesky" | custom-call | tf_op jit(solution)/shard_map/jit(cholesky)/cholesky | solution.py:9
  70.4 0.6 compare_reduce_fusion.2
  71.0 0.7 fusion.4
  71.7 2.4 %custom-call.23 = f32[1,32,32]{1,2,0:T(8,128)S(1)} custom-call(f32[1,32,32]{2,1,0:T(8,128)S(1)} %fusion.4), custom_call_target="InvertDiagBlocksLowerTriangular" | custom-call | tf_op jit(solution)/shard_map/jit(_cho_solve)/triangular_solve | solution.py:10
  74.1 37.0 %psum.44 = f32[32]{0:T(128)S(1)} all-reduce(f32[32]{0:T(128)S(1)} %broadcast_multiply_fusion), channel_id=1, replica_groups=mesh['cell'=4,'chan'=8] {'cell','chan'}, use_global_device_ids=true, to_apply=%region_5.7 | all-reduce | flops 32 | bytes 256 | tf_op jit(solution)/shard_map/psum | solution.py:28
  111.2 0.1 convolution_bitcast_fusion.1
  111.3 0.1 convolution_bitcast_fusion
  111.7 2.9 %cholesky.70 = f32[32,32]{1,0:T(8,128)S(1)} custom-call(f32[32,32]{1,0:T(8,128)S(1)} %fusion.18), custom_call_target="Cholesky" | custom-call | tf_op jit(solution)/shard_map/jit(cholesky)/cholesky | solution.py:9
  114.7 0.6 compare_reduce_fusion.1
  115.3 0.7 fusion.5
  116.0 2.4 %custom-call.24 = f32[1,32,32]{1,2,0:T(8,128)S(1)} custom-call(f32[1,32,32]{2,1,0:T(8,128)S(1)} %fusion.5), custom_call_target="InvertDiagBlocksLowerTriangular" | custom-call | tf_op jit(solution)/shard_map/jit(_cho_solve)/triangular_solve | solution.py:10
  118.4 0.1 copy.20
  118.5 1.4 multiply_add_fusion
  119.9 1.0 fusion.16
  121.0 1.0 fusion.14
  122.0 1.0 convolution_multiply_fusion
  123.0 9.4 %fusion = f32[32,1024]{1,0:T(8,128)} fusion(bf16[8192,1024]{1,0:T(8,128)(2,1)} %param.8, f32[32,8192]{1,0:T(8,128)S(1)} %fusion.14), kind=kOutput, calls=%fused_computation.7 | convolution fusion | flops 537133056 | bytes 17956864 | tf_op jit(solution)/shard_map/dot_general | solution.py:40
  132.4 15.9 %psum.46 = f32[32,32]{0,1:T(8,128)S(1)} all-reduce(f32[32,32]{0,1:T(8,128)S(1)} %convolution_multiply_fusion), channel_id=1, replica_groups=mesh['cell'=4,'chan'=8] {'cell'}, use_global_device_ids=true, to_apply=%region_7.9 | all-reduce | flops 1024 | bytes 8192 | tf_op jit(solution)/shard_map/psum | solution.py:38
  148.3 0.1 fusion.8
  148.5 2.9 %cholesky.81 = f32[32,32]{1,0:T(8,128)S(1)} custom-call(f32[32,32]{1,0:T(8,128)S(1)} %fusion.13), custom_call_target="Cholesky" | custom-call | tf_op jit(solution)/shard_map/jit(cholesky)/cholesky | solution.py:9
  151.4 0.6 compare_reduce_fusion
  152.1 0.7 fusion.6
  152.8 2.4 %custom-call.25 = f32[1,32,32]{1,2,0:T(8,128)S(1)} custom-call(f32[1,32,32]{2,1,0:T(8,128)S(1)} %fusion.6), custom_call_target="InvertDiagBlocksLowerTriangular" | custom-call | tf_op jit(solution)/shard_map/jit(_cho_solve)/triangular_solve | solution.py:10
  155.2 38.6 %all-reduce.5.cloned.1.call-done = f32[32,1024]{1,0:T(8,128)} async-done(((f32[32,1024]{1,0:T(8,128)}), f32[32,1024]{1,0:T(8,128)}) %all-reduce.5.cloned.1.call-update) | async-done | bytes 131088 | tf_op jit(solution)/shard_map/psum | solution.py:41
  193.8 1.0 multiply_add_fusion.1
  194.8 0.3 fusion.11
  195.1 0.9 fusion.9
  (42 shorter events, 0.7 us)
Async XLA Ops:
  7.2 12.5 %copy-start.3 = (f32[32,1024]{1,0:T(8,128)S(1)}, f32[32,1024]{1,0:T(8,128)}, u32[]{:S(2)}) copy-start(f32[32,1024]{1,0:T(8,128)} %param.10) | copy-start | bytes 393220
  7.2 12.8 %copy-start.1 = (f32[32,8192]{1,0:T(8,128)S(1)}, f32[32,8192]{1,0:T(8,128)}, u32[]{:S(2)}) copy-start(f32[32,8192]{1,0:T(8,128)} %param.9) | copy-start | bytes 3145732
  7.2 104.3 %copy-start.10 = (f32[32,32]{1,0:T(8,128)S(1)}, f32[32,32]{1,0:T(8,128)}, u32[]{:S(2)}) copy-start(f32[32,32]{1,0:T(8,128)} %param.13) | copy-start | bytes 12292
  7.2 111.2 %copy-start.11 = (f32[32,32]{1,0:T(8,128)S(1)}, f32[32,32]{1,0:T(8,128)}, u32[]{:S(2)}) copy-start(f32[32,32]{1,0:T(8,128)} %param.14) | copy-start | bytes 12292
  7.2 111.3 %copy-start.4 = (f32[32,8192]{1,0:T(8,128)S(1)}, f32[32,8192]{1,0:T(8,128)}, u32[]{:S(2)}) copy-start(f32[32,8192]{1,0:T(8,128)} %param.11) | copy-start | bytes 3145732
  7.2 111.3 %all-reduce.3.cloned.1.call-start = ((), (), s32[]{:S(2)}) async-start(), calls=%async_computation | async-start | bytes 2097152 | tf_op jit(solution)/shard_map/psum | solution.py:34
  19.7 174.2 %all-reduce.5.cloned.1.call-start = ((), (), s32[]{:S(2)}) async-start(), calls=%async_computation.1 | async-start | bytes 262144 | tf_op jit(solution)/shard_map/psum | solution.py:41
  111.5 82.4 %copy-start.9 = (f32[32]{0:T(128)}, f32[32]{0:T(128)S(1)}, u32[]{:S(2)}) copy-start(f32[32]{0:T(128)S(1)} %convolution_bitcast_fusion) | copy-start | bytes 388
  111.7 20.7 %copy-start.7 = (f32[32,32]{1,0:T(8,128)}, f32[32,32]{1,0:T(8,128)S(1)}, u32[]{:S(2)}) copy-start(f32[32,32]{1,0:T(8,128)S(1)} %copy.18) | copy-start | bytes 12292
  119.9 32.8 %copy-start.2 = (f32[32,8192]{1,0:T(8,128)}, f32[32,8192]{1,0:T(8,128)S(1)}, u32[]{:S(2)}) copy-start(f32[32,8192]{1,0:T(8,128)S(1)} %multiply_add_fusion) | copy-start | bytes 3145732
  119.9 73.9 %copy-start.6 = (f32[32,1024]{1,0:T(8,128)S(1)}, f32[32,1024]{1,0:T(8,128)}, u32[]{:S(2)}) copy-start(f32[32,1024]{1,0:T(8,128)} %param.12) | copy-start | bytes 393220
  122.0 74.1 %copy-start = (f32[32,8192]{1,0:T(8,128)}, f32[32,8192]{1,0:T(8,128)S(1)}, u32[]{:S(2)}) copy-start(f32[32,8192]{1,0:T(8,128)S(1)} %fusion.14) | copy-start | bytes 3145732
  148.5 47.6 %copy-start.8 = (f32[32,32]{1,0:T(8,128)}, f32[32,32]{1,0:T(8,128)S(1)}, u32[]{:S(2)}) copy-start(f32[32,32]{1,0:T(8,128)S(1)} %copy.21) | copy-start | bytes 12292
  194.8 1.3 copy-start.5
Sparse Core Ops, SparseCore 0:
  19.8 61.7 all-reduce.2
  152.2 41.5 all-reduce.4
where the time goes:
time: 203 us
  blocking collectives  99.3 us (49%)
  waiting for transfers between devices  38.7 us (19%)
  matrix products  27.5 us (14%)
  other arithmetic  22.6 us (11%)
  between operations  14.3 us (7%)
    psum x1, waiting for transfers between devices, body(): cell_summed = lax.psum(slab_cell, 'cell')  38.6 us
    psum x1, blocking collectives, body(): rhs = lax.psum(rhs_part, ('cell', 'chan'))  37 us
    psum x1, blocking collectives, body(): chan_norm = lax.psum(chan_part, 'chan')  30.4 us
    psum x1, blocking collectives, body(): cell_norm = lax.psum(cell_part, 'cell')  16 us
    psum x1, blocking collectives, body(): new_norm = lax.psum(local_gram, 'cell')  15.9 us
    dot_general x1, matrix products, body(): lax.dot_general(chan_low, slab, (((1,), (1,)), ((), ())), preferred_eleme...  12.4 us
    another operation x9, other arithmetic, spd_solve(): lower = jnp.linalg.cholesky(matrix)  10.8 us
    dot_general x1, matrix products, body(): slab_cell = jnp.dot(cell_low, slab, preferred_element_type=jnp.float32)  9.41 us
  transfers between devices with their start and end apart: 2, of which 1 were waited for; matrix products, arithmetic and copies ran while one was open for 9% of the time, Pallas kernels for 0%

commit v1 on v0

--- a/solution.py
+++ b/solution.py
@@ -35,7 +35,9 @@
     new_cell_mttkrp = cell_mttkrp + time_row[:, None] * summed / math.sqrt(all_cols)
     new_cell_factor = spd_solve(new_cell_gram, new_cell_mttkrp)
     local_gram = jnp.dot(new_cell_factor, new_cell_factor.T, precision=hi) / all_rows
-    new_norm = lax.psum(local_gram, "cell")
+    new_norm = local_gram
+    for hop in (1, 2):
+        new_norm = new_norm + lax.ppermute(new_norm, "cell", [(dev, dev ^ hop) for dev in range(4)])
     cell_low = new_cell_factor.astype(jnp.bfloat16)
     slab_cell = jnp.dot(cell_low, slab, preferred_element_type=jnp.float32)
     cell_summed = lax.psum(slab_cell, "cell")

time: 203 us -> 190 us (0.936)
  blocking collectives: 99.3 us -> 83.4 us
  starting transfers between devices: 0.08 us -> 4.43 us
    psum x1 -> x0, blocking collectives: 15.9 us -> none  [body(): new_norm = lax.psum(local_gram, 'cell')]
    ppermute x0 -> x2, starting transfers between devices: none -> 4.35 us  [body(): lax.ppermute(new_norm, 'cell', [(dev, dev ^ hop) for dev in range(4)])]
    psum x1, waiting for transfers between devices: 38.6 us -> 35 us  [body(): cell_summed = lax.psum(slab_cell, 'cell')]
  transfers between devices with their start and end apart: 2 -> 4, of which waited for: 1 -> 2; matrix products, arithmetic and copies ran while one was open for 9% -> 17% of each run, Pallas kernels for 0% -> 0%
where the time goes in v1:
time: 190 us; the launch traced here: 189 us
  blocking collectives  83.4 us (44%)
  waiting for transfers between devices  36.7 us (19%)
  matrix products  27.5 us (14%)
  other arithmetic  22.6 us (12%)
  between operations  14.3 us (8%)
  starting transfers between devices  4.43 us (2%)
    psum x1, blocking collectives, body(): rhs = lax.psum(rhs_part, ('cell', 'chan'))  37 us
    psum x1, waiting for transfers between devices, body(): cell_summed = lax.psum(slab_cell, 'cell')  35 us
    psum x1, blocking collectives, body(): chan_norm = lax.psum(chan_part, 'chan')  30.4 us
    psum x1, blocking collectives, body(): cell_norm = lax.psum(cell_part, 'cell')  16 us
    dot_general x1, matrix products, body(): lax.dot_general(chan_low, slab, (((1,), (1,)), ((), ())), preferred_eleme...  12.4 us
    another operation x9, other arithmetic, spd_solve(): lower = jnp.linalg.cholesky(matrix)  10.8 us
    dot_general x1, matrix products, body(): slab_cell = jnp.dot(cell_low, slab, preferred_element_type=jnp.float32)  9.41 us
    another operation x6, other arithmetic, spd_solve(): return jax.scipy.linalg.cho_solve((lower, True), right)  9.26 us
  transfers between devices with their start and end apart: 4, of which 2 were waited for; matrix products, arithmetic and copies ran while one was open for 17% of the time, Pallas kernels for 0%

profile of v1, /device:TPU:0, one launch (start us, length us, event | category | flops | bytes accessed | tf_op | source)
XLA Modules:
  0.0 189.4 jit_solution(10480552552941833339)
XLA Ops:
  7.3 12.4 %multiply_reduce_fusion = (f32[32]{0:T(128)S(1)}, f32[32,8192]{1,0:T(8,128)}) fusion(f32[32,8192]{1,0:T(8,128)} %param.9, bf16[8192,1024]{1,0:T(8,128)(2,1)} %param.8, f32[32,1024]{1,0:T(8,128)} %param.10), kind=kOutput, calls=%fused_computation.6 | convolution fusion | flops 537427968 | bytes 19005568 | tf_op jit(solution)/shard_map/dot_general | solution.py:22
  19.7 0.2 convolution_multiply_fusion.1
  20.0 1.0 convolution_multiply_fusion.2
  21.0 30.4 %psum.36 = f32[32,32]{0,1:T(8,128)S(1)} all-reduce(f32[32,32]{0,1:T(8,128)S(1)} %convolution_multiply_fusion.1), channel_id=1, replica_groups=mesh['cell'=4,'chan'=8] {'chan'}, use_global_device_ids=true, to_apply=%region_1.0 | all-reduce | flops 1024 | bytes 8192 | tf_op jit(solution)/shard_map/psum | solution.py:30
  51.3 16.0 %psum.35 = f32[32,32]{0,1:T(8,128)S(1)} all-reduce(f32[32,32]{0,1:T(8,128)S(1)} %convolution_multiply_fusion.2), channel_id=1, replica_groups=mesh['cell'=4,'chan'=8] {'cell'}, use_global_device_ids=true, to_apply=%region_0.0 | all-reduce | flops 1024 | bytes 8192 | tf_op jit(solution)/shard_map/psum | solution.py:29
  67.4 2.9 %cholesky.59 = f32[32,32]{1,0:T(8,128)S(1)} custom-call(f32[32,32]{1,0:T(8,128)S(1)} %fusion.21), custom_call_target="Cholesky" | custom-call | tf_op jit(solution)/shard_map/jit(cholesky)/cholesky | solution.py:9
  70.4 0.6 compare_reduce_fusion.2
  71.0 0.7 fusion.4
  71.7 2.4 %custom-call.23 = f32[1,32,32]{1,2,0:T(8,128)S(1)} custom-call(f32[1,32,32]{2,1,0:T(8,128)S(1)} %fusion.4), custom_call_target="InvertDiagBlocksLowerTriangular" | custom-call | tf_op jit(solution)/shard_map/jit(_cho_solve)/triangular_solve | solution.py:10
  74.1 37.0 %psum.37 = f32[32]{0:T(128)S(1)} all-reduce(f32[32]{0:T(128)S(1)} %broadcast_multiply_fusion), channel_id=1, replica_groups=mesh['cell'=4,'chan'=8] {'cell','chan'}, use_global_device_ids=true, to_apply=%region_5.7 | all-reduce | flops 32 | bytes 256 | tf_op jit(solution)/shard_map/psum | solution.py:28
  111.2 0.1 convolution_bitcast_fusion.1
  111.3 0.1 convolution_bitcast_fusion
  111.7 2.9 %cholesky.70 = f32[32,32]{1,0:T(8,128)S(1)} custom-call(f32[32,32]{1,0:T(8,128)S(1)} %fusion.18), custom_call_target="Cholesky" | custom-call | tf_op jit(solution)/shard_map/jit(cholesky)/cholesky | solution.py:9
  114.7 0.6 compare_reduce_fusion.1
  115.3 0.7 fusion.5
  116.0 2.4 %custom-call.24 = f32[1,32,32]{1,2,0:T(8,128)S(1)} custom-call(f32[1,32,32]{2,1,0:T(8,128)S(1)} %fusion.5), custom_call_target="InvertDiagBlocksLowerTriangular" | custom-call | tf_op jit(solution)/shard_map/jit(_cho_solve)/triangular_solve | solution.py:10
  118.4 1.4 multiply_add_fusion
  119.9 1.0 fusion.16
  120.9 1.0 fusion.14
  121.9 1.0 convolution_multiply_fusion
  122.9 2.3 %collective-permute-start = (f32[32,32]{0,1:T(8,128)S(1)}, f32[32,32]{0,1:T(8,128)S(1)}, u32[]{:S(2)}, u32[]{:S(2)}) collective-permute-start(f32[32,32]{0,1:T(8,128)S(1)} %convolution_multiply_fusion), channel_id=1, source_target_pairs={{0,8},{8,0},{16,24},{24,16},{1,9},{9,1},{17,25},{25,17},{2,10},{10... | collective-permute-start | bytes 12296 | tf_op jit(solution)/shard_map/ppermute | solution.py:40
  125.3 1.6 collective-permute-done
  127.0 2.0 %collective-permute-start.1 = (f32[32,32]{0,1:T(8,128)S(1)}, f32[32,32]{0,1:T(8,128)S(1)}, u32[]{:S(2)}, u32[]{:S(2)}) collective-permute-start(f32[32,32]{0,1:T(8,128)S(1)} %add.55), channel_id=1, source_target_pairs={{0,16},{8,24},{16,0},{24,8},{1,17},{9,25},{17,1},{25,9},{2,18},{10... | collective-permute-start | bytes 12296 | tf_op jit(solution)/shard_map/ppermute | solution.py:40
  129.0 9.4 %fusion = f32[32,1024]{1,0:T(8,128)} fusion(bf16[8192,1024]{1,0:T(8,128)(2,1)} %param.8, f32[32,8192]{1,0:T(8,128)S(1)} %fusion.14), kind=kOutput, calls=%fused_computation.7 | convolution fusion | flops 537133056 | bytes 17956864 | tf_op jit(solution)/shard_map/dot_general | solution.py:42
  138.6 2.9 %cholesky.81 = f32[32,32]{1,0:T(8,128)S(1)} custom-call(f32[32,32]{1,0:T(8,128)S(1)} %fusion.13), custom_call_target="Cholesky" | custom-call | tf_op jit(solution)/shard_map/jit(cholesky)/cholesky | solution.py:9
  141.6 0.6 compare_reduce_fusion
  142.2 0.7 fusion.6
  142.9 2.4 %custom-call.25 = f32[1,32,32]{1,2,0:T(8,128)S(1)} custom-call(f32[1,32,32]{2,1,0:T(8,128)S(1)} %fusion.6), custom_call_target="InvertDiagBlocksLowerTriangular" | custom-call | tf_op jit(solution)/shard_map/jit(_cho_solve)/triangular_solve | solution.py:10
  145.3 35.0 %all-reduce.5.cloned.1.call-done = f32[32,1024]{1,0:T(8,128)} async-done(((f32[32,1024]{1,0:T(8,128)}), f32[32,1024]{1,0:T(8,128)}) %all-reduce.5.cloned.1.call-update) | async-done | bytes 131088 | tf_op jit(solution)/shard_map/psum | solution.py:43
  180.3 1.0 multiply_add_fusion.1
  181.3 0.3 fusion.11
  181.6 0.9 fusion.9
  (46 shorter events, 0.8 us)
Async XLA Ops:
  7.2 12.5 %copy-start.3 = (f32[32,1024]{1,0:T(8,128)S(1)}, f32[32,1024]{1,0:T(8,128)}, u32[]{:S(2)}) copy-start(f32[32,1024]{1,0:T(8,128)} %param.10) | copy-start | bytes 393220
  7.2 12.8 %copy-start.1 = (f32[32,8192]{1,0:T(8,128)S(1)}, f32[32,8192]{1,0:T(8,128)}, u32[]{:S(2)}) copy-start(f32[32,8192]{1,0:T(8,128)} %param.9) | copy-start | bytes 3145732
  7.2 104.3 %copy-start.10 = (f32[32,32]{1,0:T(8,128)S(1)}, f32[32,32]{1,0:T(8,128)}, u32[]{:S(2)}) copy-start(f32[32,32]{1,0:T(8,128)} %param.13) | copy-start | bytes 12292
  7.2 111.2 %copy-start.4 = (f32[32,8192]{1,0:T(8,128)S(1)}, f32[32,8192]{1,0:T(8,128)}, u32[]{:S(2)}) copy-start(f32[32,8192]{1,0:T(8,128)} %param.11) | copy-start | bytes 3145732
  7.2 118.0 %copy-start.11 = (f32[32,32]{1,0:T(8,128)S(1)}, f32[32,32]{1,0:T(8,128)}, u32[]{:S(2)}) copy-start(f32[32,32]{1,0:T(8,128)} %param.14) | copy-start | bytes 12292
  7.2 111.2 %all-reduce.3.cloned.1.call-start = ((), (), s32[]{:S(2)}) async-start(), calls=%async_computation | async-start | bytes 2097152 | tf_op jit(solution)/shard_map/psum | solution.py:34
  19.7 160.6 %all-reduce.5.cloned.1.call-start = ((), (), s32[]{:S(2)}) async-start(), calls=%async_computation.1 | async-start | bytes 262144 | tf_op jit(solution)/shard_map/psum | solution.py:43
  111.5 68.8 %copy-start.9 = (f32[32]{0:T(128)}, f32[32]{0:T(128)S(1)}, u32[]{:S(2)}) copy-start(f32[32]{0:T(128)S(1)} %convolution_bitcast_fusion) | copy-start | bytes 388
  111.7 26.7 %copy-start.7 = (f32[32,32]{1,0:T(8,128)}, f32[32,32]{1,0:T(8,128)S(1)}, u32[]{:S(2)}) copy-start(f32[32,32]{1,0:T(8,128)S(1)} %copy.18) | copy-start | bytes 12292
  119.8 18.8 %copy-start.2 = (f32[32,8192]{1,0:T(8,128)}, f32[32,8192]{1,0:T(8,128)S(1)}, u32[]{:S(2)}) copy-start(f32[32,8192]{1,0:T(8,128)S(1)} %multiply_add_fusion) | copy-start | bytes 3145732
  119.9 60.4 %copy-start.6 = (f32[32,1024]{1,0:T(8,128)S(1)}, f32[32,1024]{1,0:T(8,128)}, u32[]{:S(2)}) copy-start(f32[32,1024]{1,0:T(8,128)} %param.12) | copy-start | bytes 393220
  121.9 60.6 %copy-start = (f32[32,8192]{1,0:T(8,128)}, f32[32,8192]{1,0:T(8,128)S(1)}, u32[]{:S(2)}) copy-start(f32[32,8192]{1,0:T(8,128)S(1)} %fusion.14) | copy-start | bytes 3145732
  122.9 4.1 %collective-permute-start = (f32[32,32]{0,1:T(8,128)S(1)}, f32[32,32]{0,1:T(8,128)S(1)}, u32[]{:S(2)}, u32[]{:S(2)}) collective-permute-start(f32[32,32]{0,1:T(8,128)S(1)} %convolution_multiply_fusion), channel_id=1, source_target_pairs={{0,8},{8,0},{16,24},{24,16},{1,9},{9,1},{17,25},{25,17},{2,10},{10... | collective-permute-start | bytes 12296 | tf_op jit(solution)/shard_map/ppermute | solution.py:40
  127.0 11.5 %collective-permute-start.1 = (f32[32,32]{0,1:T(8,128)S(1)}, f32[32,32]{0,1:T(8,128)S(1)}, u32[]{:S(2)}, u32[]{:S(2)}) collective-permute-start(f32[32,32]{0,1:T(8,128)S(1)} %add.55), channel_id=1, source_target_pairs={{0,16},{8,24},{16,0},{24,8},{1,17},{9,25},{17,1},{25,9},{2,18},{10... | collective-permute-start | bytes 12296 | tf_op jit(solution)/shard_map/ppermute | solution.py:40
  138.6 43.9 %copy-start.8 = (f32[32,32]{1,0:T(8,128)}, f32[32,32]{1,0:T(8,128)S(1)}, u32[]{:S(2)}) copy-start(f32[32,32]{1,0:T(8,128)S(1)} %copy.21) | copy-start | bytes 12292
  181.3 1.3 copy-start.5
Sparse Core Ops, SparseCore 0:
  19.8 61.7 all-reduce.2
  138.5 41.6 all-reduce.4
